TPU v7x, 32 devices: a whole 2x2x4 slice. The times are simulated.
32 devices in a mesh: dp: 8 (over z, x), tensor: 4 (over y, core).
Axes of the slice: x: 2, y: 2, z: 4, core: 2. Of those that a mesh axis runs over, the one named last changes fastest.
Arguments:
- block_in: float32 [4096, 1024], P(('dp', 'tensor')), may hold values from -20 to 20
- in_proj: bfloat16 [3, 1024, 1024], P(None, 'dp', 'tensor'), may hold values from -4 to 4
- in_bias: bfloat16 [2, 16, 64], P(None, 'tensor', 'dp'), may hold values from -3 to 3
- out_proj: bfloat16 [1024, 1024], P('tensor', 'dp'), may hold values from -3 to 3
- up_proj: bfloat16 [1024, 4096], P('dp', 'tensor'), may hold values from -0.1875 to 0.1875
- up_bias: bfloat16 [16, 256], P('tensor', 'dp'), may hold values from -3 to 3
- down_proj: bfloat16 [4096, 1024], P('tensor', 'dp'), may hold values from -0.1875 to 0.1875
- norm_params: bfloat16 [6, 1024], P(None, 'dp'), may hold values from -2 to 2
- grad_out: float32 [4096, 1024], P(('dp', 'tensor')), may hold values from -6 to 6
Outputs:
- block_out: float32 [4096, 1024], P(('dp', 'tensor'))
- grad_in: float32 [4096, 1024], P(('dp', 'tensor'))
- grad_in_proj: float32 [3, 1024, 1024], P(None, 'dp', 'tensor')
- grad_in_bias: float32 [2, 16, 64], P(None, 'tensor', 'dp')
- grad_out_proj: float32 [1024, 1024], P('tensor', 'dp')
- grad_up_proj: float32 [1024, 4096], P('dp', 'tensor')
- grad_up_bias: float32 [16, 256], P('tensor', 'dp')
- grad_down_proj: float32 [4096, 1024], P('tensor', 'dp')
- grad_norm_params: float32 [6, 1024], P(None, ('dp', 'tensor'))
All inputs are finite; a program needn't handle non-finite values.
Results may differ from a plain program's by a relative error of at most 0.015.
The roundings to bfloat16 on the way count: a program that leaves them out, or rounds other values in their place, can miss the bound.
Values may be sent and summed in bfloat16 or wider, within the bound.
A program may use at most 128 MiB of HBM per device.

v0:
```python
import math

import jax
import jax.numpy as jnp
from jax import lax
from jax.sharding import PartitionSpec as P


def layer_norm(rows, gain, shift):
    center = rows - jnp.mean(rows, -1, keepdims=True)
    var = jnp.mean(center * center, -1, keepdims=True)
    return center * lax.rsqrt(var + 1e-05) * gain + shift


def gelu_curve(value):
    return 0.5 * value * (1.0 + jnp.tanh(0.7978845608 * (value + 0.044715 * value * value * value)))


def block_scores(rows_q, keys, start, scale, seq_len):
    block_rows = rows_q.shape[0]
    scores = jnp.einsum("qhe,khe->hqk", rows_q, keys, preferred_element_type=jnp.float32) * scale
    positions = start + jnp.arange(block_rows, dtype=jnp.int32)
    allowed = jnp.arange(seq_len, dtype=jnp.int32)[None, :] <= positions[:, None]
    return (jnp.where(allowed[None], scores, -1e30), allowed)


def attend(query, keys, values):
    seq_len, heads, head_dim = query.shape
    block_rows = min(512, seq_len)
    count = seq_len // block_rows
    scale = 1.0 / math.sqrt(head_dim)
    starts = jnp.arange(count, dtype=jnp.int32) * block_rows

    def one_block(item):
        rows_q, start = item
        scores, allowed = block_scores(rows_q, keys, start, scale, seq_len)
        peak = jnp.max(scores, -1, keepdims=True)
        expo = jnp.exp(scores - peak)
        total = jnp.sum(expo, -1, keepdims=True)
        probs = (expo / total).astype(jnp.bfloat16)
        out = jnp.einsum("hqk,khe->qhe", probs, values, preferred_element_type=jnp.float32).astype(
            jnp.bfloat16
        )
        return (out, (peak + jnp.log(total))[:, :, 0])

    outs, logs = lax.map(one_block, (query.reshape(count, block_rows, heads, head_dim), starts))
    return (outs.reshape(seq_len, heads, head_dim), logs)


def attend_back(query, keys, values, mixed, grad_mixed, log_total):
    seq_len, heads, head_dim = query.shape
    block_rows = min(512, seq_len)
    count = seq_len // block_rows
    scale = 1.0 / math.sqrt(head_dim)
    starts = jnp.arange(count, dtype=jnp.int32) * block_rows
    row_dot = jnp.sum(grad_mixed.astype(jnp.float32) * mixed.astype(jnp.float32), -1)

    def step(carry, item):
        grad_k, grad_v = carry
        rows_q, rows_g, rows_log, rows_dot, start = item
        scores, allowed = block_scores(rows_q, keys, start, scale, seq_len)
        probs = jnp.where(allowed[None], jnp.exp(scores - rows_log[:, :, None]), 0.0)
        probs_low = probs.astype(jnp.bfloat16)
        grad_v = grad_v + jnp.einsum(
            "hqk,qhe->khe", probs_low, rows_g, preferred_element_type=jnp.float32
        )
        grad_p = jnp.einsum("qhe,khe->hqk", rows_g, values, preferred_element_type=jnp.float32)
        grad_s = (probs * (grad_p - jnp.transpose(rows_dot)[:, :, None])).astype(jnp.bfloat16)
        grad_q = (
            jnp.einsum("hqk,khe->qhe", grad_s, keys, preferred_element_type=jnp.float32) * scale
        )
        grad_k = (
            grad_k
            + jnp.einsum("hqk,qhe->khe", grad_s, rows_q, preferred_element_type=jnp.float32) * scale
        )
        return ((grad_k, grad_v), grad_q)

    zeros = jnp.zeros((seq_len, heads, head_dim), jnp.float32)
    items = (
        query.reshape(count, block_rows, heads, head_dim),
        grad_mixed.reshape(count, block_rows, heads, head_dim),
        log_total,
        row_dot.reshape(count, block_rows, heads),
        starts,
    )
    (grad_k, grad_v), grad_qs = lax.scan(step, (zeros, zeros), items)
    return (grad_qs.reshape(seq_len, heads, head_dim), grad_k, grad_v)


def body(block_in, in_proj, in_bias, out_proj, up_proj, up_bias, down_proj, norm_params, grad_out):
    proj_in, bias_in, proj_out, norms = (
        lax.all_gather(in_proj, "dp", axis=1, tiled=True),
        lax.all_gather(in_bias, "dp", axis=2, tiled=True),
        lax.all_gather(out_proj, "dp", axis=1, tiled=True),
        lax.all_gather(norm_params, "dp", axis=1, tiled=True),
    )
    norms = norms.astype(jnp.float32)
    gain_one, shift_one, bias_attn, gain_two, shift_two, bias_feed = [norms[i] for i in range(6)]
    heads_here = bias_in.shape[1]
    head_dim = bias_in.shape[2]
    columns = heads_here * head_dim
    normed_one = layer_norm(block_in, gain_one, shift_one).astype(jnp.bfloat16)
    whole_one = lax.all_gather(normed_one, "tensor", axis=0, tiled=True)
    seq_len = whole_one.shape[0]
    projected = jnp.einsum("ld,jdc->jlc", whole_one, proj_in, preferred_element_type=jnp.float32)
    bias_flat = bias_in.astype(jnp.float32).reshape(2, columns)
    query = (
        (projected[0] + bias_flat[0]).astype(jnp.bfloat16).reshape(seq_len, heads_here, head_dim)
    )
    keys = projected[1].astype(jnp.bfloat16).reshape(seq_len, heads_here, head_dim)
    values = (
        (projected[2] + bias_flat[1]).astype(jnp.bfloat16).reshape(seq_len, heads_here, head_dim)
    )
    mixed, log_total = attend(query, keys, values)
    mixed_flat = mixed.reshape(seq_len, columns)
    attn_part = jnp.dot(mixed_flat, proj_out, preferred_element_type=jnp.float32)
    attn_sum = lax.psum_scatter(attn_part, "tensor", scatter_dimension=0, tiled=True)
    middle = block_in + attn_sum + bias_attn
    normed_two = layer_norm(middle, gain_two, shift_two).astype(jnp.bfloat16)
    whole_two = lax.all_gather(normed_two, "tensor", axis=0, tiled=True)
    proj_up, bias_up, proj_down = (
        lax.all_gather(up_proj, "dp", axis=0, tiled=True),
        lax.all_gather(up_bias, "dp", axis=1, tiled=True),
        lax.all_gather(down_proj, "dp", axis=1, tiled=True),
    )
    hidden_pre = jnp.dot(whole_two, proj_up, preferred_element_type=jnp.float32) + bias_up.astype(
        jnp.float32
    ).reshape(-1)
    hidden = gelu_curve(hidden_pre).astype(jnp.bfloat16)
    feed_part = jnp.dot(hidden, proj_down, preferred_element_type=jnp.float32)
    feed_sum = lax.psum_scatter(feed_part, "tensor", scatter_dimension=0, tiled=True)
    block_out = middle + feed_sum + bias_feed
    grad_low = grad_out.astype(jnp.bfloat16)
    whole_grad = lax.all_gather(grad_low, "tensor", axis=0, tiled=True)
    grad_down = jnp.einsum("lf,ld->fd", hidden, whole_grad, preferred_element_type=jnp.float32)
    grad_hidden = jnp.einsum("ld,fd->lf", whole_grad, proj_down, preferred_element_type=jnp.float32)
    _, curve_back = jax.vjp(gelu_curve, hidden_pre)
    grad_pre = curve_back(grad_hidden)[0]
    grad_upb = jnp.sum(grad_pre, 0).reshape(bias_up.shape)
    grad_pre_low = grad_pre.astype(jnp.bfloat16)
    grad_up = jnp.einsum("ld,lf->df", whole_two, grad_pre_low, preferred_element_type=jnp.float32)
    two_part = jnp.einsum("lf,df->ld", grad_pre_low, proj_up, preferred_element_type=jnp.float32)
    normed_two_grad = lax.psum_scatter(two_part, "tensor", scatter_dimension=0, tiled=True)
    _, norm_back_two = jax.vjp(layer_norm, middle, gain_two, shift_two)
    grad_mid_norm, grad_gain_two, grad_shift_two = norm_back_two(normed_two_grad)
    grad_middle = grad_out + grad_mid_norm
    middle_low = grad_middle.astype(jnp.bfloat16)
    whole_mid = lax.all_gather(middle_low, "tensor", axis=0, tiled=True)
    grad_proj_out = jnp.einsum(
        "lc,ld->cd", mixed_flat, whole_mid, preferred_element_type=jnp.float32
    )
    grad_mixed = jnp.einsum("ld,cd->lc", whole_mid, proj_out, preferred_element_type=jnp.float32)
    grad_mixed = grad_mixed.astype(jnp.bfloat16).reshape(seq_len, heads_here, head_dim)
    grad_q, grad_k, grad_v = attend_back(query, keys, values, mixed, grad_mixed, log_total)
    grad_bias_in = jnp.stack([jnp.sum(grad_q, 0), jnp.sum(grad_v, 0)])
    grad_proj = (
        jnp.stack([grad_q, grad_k, grad_v]).reshape(3, seq_len, columns).astype(jnp.bfloat16)
    )
    grad_in_w = jnp.einsum("ld,jlc->jdc", whole_one, grad_proj, preferred_element_type=jnp.float32)
    one_part = jnp.einsum("jlc,jdc->ld", grad_proj, proj_in, preferred_element_type=jnp.float32)
    normed_one_grad = lax.psum_scatter(one_part, "tensor", scatter_dimension=0, tiled=True)
    _, norm_back_one = jax.vjp(layer_norm, block_in, gain_one, shift_one)
    grad_in_norm, grad_gain_one, grad_shift_one = norm_back_one(normed_one_grad)
    grad_in = grad_middle + grad_in_norm
    norm_terms = jnp.stack(
        [
            grad_gain_one,
            grad_shift_one,
            jnp.sum(grad_middle, 0),
            grad_gain_two,
            grad_shift_two,
            jnp.sum(grad_out, 0),
        ]
    )
    grad_norms = lax.psum_scatter(norm_terms, ("dp", "tensor"), scatter_dimension=1, tiled=True)
    summed = (
        lax.psum_scatter(grad_in_w, "dp", scatter_dimension=1, tiled=True),
        lax.psum_scatter(grad_bias_in, "dp", scatter_dimension=2, tiled=True),
        lax.psum_scatter(grad_proj_out, "dp", scatter_dimension=1, tiled=True),
        lax.psum_scatter(grad_up, "dp", scatter_dimension=0, tiled=True),
        lax.psum_scatter(grad_upb, "dp", scatter_dimension=1, tiled=True),
        lax.psum_scatter(grad_down, "dp", scatter_dimension=1, tiled=True),
    )
    grad_in_proj, grad_in_bias, grad_out_proj, grad_up_proj, grad_up_bias, grad_down_proj = summed
    return (
        block_out,
        grad_in,
        grad_in_proj,
        grad_in_bias,
        grad_out_proj,
        grad_up_proj,
        grad_up_bias,
        grad_down_proj,
        grad_norms,
    )


def solution(mesh):
    return jax.shard_map(
        body,
        mesh=mesh,
        in_specs=(
            P(("dp", "tensor"), None),
            P(None, "dp", "tensor"),
            P(None, "tensor", "dp"),
            P("tensor", "dp"),
            P("dp", "tensor"),
            P("tensor", "dp"),
            P("tensor", "dp"),
            P(None, "dp"),
            P(("dp", "tensor"), None),
        ),
        out_specs=(
            P(("dp", "tensor"), None),
            P(("dp", "tensor"), None),
            P(None, "dp", "tensor"),
            P(None, "tensor", "dp"),
            P("tensor", "dp"),
            P("dp", "tensor"),
            P("tensor", "dp"),
            P("tensor", "dp"),
            P(None, ("dp", "tensor")),
        ),
        check_vma=False,
    )
```

profile of v0, /device:TPU:0, one launch (start us, length us, event | category | flops | bytes accessed | tf_op | source)
XLA Modules:
  0.0 957.6 jit_solution(7907969313506265085)
XLA Ops:
  9.7 28.1 %all_gather.33 = bf16[6,1024]{1,0:T(8,128)(2,1)S(1)} all-gather(bf16[6,128]{1,0:T(8,128)(2,1)} %param.16), channel_id=1, replica_groups=mesh['dp'=8,'tensor'=4] {'dp'}, dimensions={1}, use_global_device_ids=true | all-gather | bytes 13824 | tf_op jit(solution)/shard_map/all_gather | solution.py:95
  40.8 30.7 %all_gather.36 = bf16[2,4,64]{1,0,2:T(2,128)(2,1)S(1)} all-gather(bf16[2,4,8]{1,0,2:T(2,128)(2,1)S(1)} %copy.60), channel_id=1, replica_groups=mesh['dp'=8,'tensor'=4] {'dp'}, dimensions={2}, use_global_device_ids=true | all-gather | bytes 1152 | tf_op jit(solution)/shard_map/all_gather | solution.py:93
  71.8 29.2 %all_gather.37 = bf16[256,1024]{1,0:T(8,128)(2,1)S(1)} all-gather(bf16[256,128]{1,0:T(8,128)(2,1)S(1)} %copy-done.12), channel_id=1, replica_groups=mesh['dp'=8,'tensor'=4] {'dp'}, dimensions={1}, use_global_device_ids=true | all-gather | bytes 589824 | tf_op jit(solution)/shard_map/all_gather | solution.py:94
  101.1 6.3 all-gather.11.cloned.1.call-done
  117.0 29.2 %reduce-scatter.16.cloned.1.call-done = f32[128,1024]{1,0:T(8,128)} async-done(((f32[512,1024]{1,0:T(8,128)}), f32[128,1024]{1,0:T(8,128)}) %reduce-scatter.16.cloned.1.call-update) | async-done | bytes 524304 | tf_op jit(solution)/shard_map/reduce_scatter | solution.py:117
  150.1 20.5 %all-gather = bf16[8,32,4]{1,2,0:T(4,128)(2,1)S(1)} all-gather(bf16[1,32,4]{1,2,0:T(4,128)(2,1)S(1)} %bitcast.124), channel_id=1, replica_groups=mesh['dp'=8,'tensor'=4] {'dp'}, dimensions={0}, use_global_device_ids=true | all-gather | bytes 2304 | tf_op jit(solution)/shard_map/all_gather | solution.py:123
  170.7 26.7 %all-gather.15.cloned.1.call-done = bf16[1024,1024]{1,0:T(8,128)(2,1)} async-done(((bf16[128,1024]{1,0:T(8,128)(2,1)}), bf16[1024,1024]{1,0:T(8,128)(2,1)}) %all-gather.15.cloned.1.call-update) | async-done | bytes 2097168 | tf_op jit(solution)/shard_map/all_gather | solution.py:122
  197.4 17.2 %all-gather.13.cloned.1.call-done = bf16[512,1024]{1,0:T(8,128)(2,1)} async-done(((bf16[128,1024]{1,0:T(8,128)(2,1)}), bf16[512,1024]{1,0:T(8,128)(2,1)}) %all-gather.13.cloned.1.call-update) | async-done | bytes 1048592 | tf_op jit(solution)/shard_map/all_gather | solution.py:120
  219.2 14.2 %all-gather.19.cloned.1.call-done = bf16[512,1024]{1,0:T(8,128)(2,1)} async-done(((bf16[128,1024]{1,0:T(8,128)(2,1)}), bf16[512,1024]{1,0:T(8,128)(2,1)}) %all-gather.19.cloned.1.call-update) | async-done | bytes 1048592 | tf_op jit(solution)/shard_map/all_gather | solution.py:134
  233.4 52.4 %all-gather.17.cloned.1.call-done = bf16[1024,1024]{1,0:T(8,128)(2,1)} async-done(((bf16[1024,128]{1,0:T(8,128)(2,1)}), bf16[1024,1024]{1,0:T(8,128)(2,1)}) %all-gather.17.cloned.1.call-update) | async-done | bytes 2097168 | tf_op jit(solution)/shard_map/all_gather | solution.py:124
  285.8 5.5 fusion.37
  295.2 5.0 fusion.35
  300.3 24.2 %reduce-scatter.20.cloned.1.call-done = f32[128,1024]{1,0:T(8,128)} async-done(((f32[512,1024]{1,0:T(8,128)}), f32[128,1024]{1,0:T(8,128)}) %reduce-scatter.20.cloned.1.call-update) | async-done | bytes 524304 | tf_op jit(solution)/shard_map/reduce_scatter | solution.py:143
  325.9 32.4 %reduce-scatter.18.cloned.1.call-done = f32[128,1024]{1,0:T(8,128)} async-done(((f32[512,1024]{1,0:T(8,128)}), f32[128,1024]{1,0:T(8,128)}) %reduce-scatter.18.cloned.1.call-update) | async-done | bytes 524304 | tf_op jit(solution)/shard_map/reduce_scatter | solution.py:131
  361.4 16.8 %all-gather.21.cloned.1.call-done = bf16[512,1024]{1,0:T(8,128)(2,1)} async-done(((bf16[128,1024]{1,0:T(8,128)(2,1)}), bf16[512,1024]{1,0:T(8,128)(2,1)}) %all-gather.21.cloned.1.call-update) | async-done | bytes 1048592 | tf_op jit(solution)/shard_map/all_gather | solution.py:148
  392.0 30.4 %reduce-scatter.22.cloned.1.call-done = f32[128,1024]{1,0:T(8,128)} async-done(((f32[512,1024]{1,0:T(8,128)}), f32[128,1024]{1,0:T(8,128)}) %reduce-scatter.22.cloned.1.call-update) | async-done | bytes 524304 | tf_op jit(solution)/shard_map/reduce_scatter | solution.py:161
  430.4 5.1 fusion.34
  442.2 45.8 %reduce-scatter.32.cloned.1.call-done = f32[32,4]{1,0:T(8,128)} async-done(((f32[256,4]{1,0:T(8,128)}), f32[32,4]{1,0:T(8,128)}) %reduce-scatter.32.cloned.1.call-update) | async-done | bytes 528
  489.4 19.5 %all-reduce = f32[2,4,64]{2,1,0:T(4,128)S(1)} all-reduce(f32[2,4,64]{2,1,0:T(4,128)S(1)} %pad_maximum_fusion.3), channel_id=7, replica_groups=mesh['dp'=8,'tensor'=4] {'dp'}, use_global_device_ids=true, to_apply=%region_18.19.clone | all-reduce | flops 512 | bytes 4096
  510.8 114.4 %reduce-scatter.34.cloned.1.call-done = f32[32,6]{1,0:T(8,128)} async-done(((f32[1024,6]{1,0:T(8,128)}), f32[32,6]{1,0:T(8,128)}) %reduce-scatter.34.cloned.1.call-update) | async-done | bytes 784
  626.5 72.9 %reduce-scatter.24.cloned.1.call-done = f32[3,128,256]{1,2,0:T(8,128)} async-done(((f32[3,1024,256]{1,2,0:T(8,128)}), f32[3,128,256]{1,2,0:T(8,128)}) %reduce-scatter.24.cloned.1.call-update) | async-done | bytes 393232 | tf_op jit(solution)/shard_map/reduce_scatter | solution.py:177
  701.3 66.0 %reduce-scatter.26.cloned.1.call-done = f32[256,128]{1,0:T(8,128)} async-done(((f32[256,1024]{1,0:T(8,128)}), f32[256,128]{1,0:T(8,128)}) %reduce-scatter.26.cloned.1.call-update) | async-done | bytes 131088 | tf_op jit(solution)/shard_map/reduce_scatter | solution.py:179
  767.3 91.7 %reduce-scatter.30.cloned.1.call-done = f32[1024,128]{1,0:T(8,128)} async-done(((f32[1024,1024]{1,0:T(8,128)}), f32[1024,128]{1,0:T(8,128)}) %reduce-scatter.30.cloned.1.call-update) | async-done | bytes 524304 | tf_op jit(solution)/shard_map/reduce_scatter | solution.py:182
  859.0 92.0 %reduce-scatter.28.cloned.1.call-done = f32[128,1024]{1,0:T(8,128)} async-done(((f32[1024,1024]{1,0:T(8,128)}), f32[128,1024]{1,0:T(8,128)}) %reduce-scatter.28.cloned.1.call-update) | async-done | bytes 524304 | tf_op jit(solution)/shard_map/reduce_scatter | solution.py:180
  (137 shorter events, 66.3 us)
Async XLA Ops:
  7.2 32.6 %copy-start.11 = (bf16[3,128,256]{2,1,0:T(8,128)(2,1)S(1)}, bf16[3,128,256]{2,1,0:T(8,128)(2,1)}, u32[]{:S(2)}) copy-start(bf16[3,128,256]{2,1,0:T(8,128)(2,1)} %param.10) | copy-start | bytes 589828
  7.2 33.5 %copy-start.13 = (bf16[2,4,8]{2,1,0:T(4,128)(2,1)S(1)}, bf16[2,4,8]{2,1,0:T(4,128)(2,1)}, u32[]{:S(2)}) copy-start(bf16[2,4,8]{2,1,0:T(4,128)(2,1)} %param.11) | copy-start | bytes 388
  7.2 64.6 %copy-start.12 = (bf16[256,128]{1,0:T(8,128)(2,1)S(1)}, bf16[256,128]{1,0:T(8,128)(2,1)}, u32[]{:S(2)}) copy-start(bf16[256,128]{1,0:T(8,128)(2,1)} %param.12) | copy-start | bytes 196612
  7.2 93.8 %all-gather.9.cloned.1.call-start = ((), (), s32[]{:S(2)}) async-start(), calls=%async_computation.10 | async-start | bytes 1310720 | tf_op jit(solution)/shard_map/all_gather | solution.py:103
  39.8 67.6 %all-gather.11.cloned.1.call-start = ((), (), s32[]{:S(2)}) async-start(), calls=%async_computation.11 | async-start | bytes 1769472 | tf_op jit(solution)/shard_map/all_gather | solution.py:92
  40.7 105.5 %reduce-scatter.16.cloned.1.call-start = ((), (), s32[]{:S(2)}) async-start(), calls=%async_computation.12 | async-start | bytes 2621440 | tf_op jit(solution)/shard_map/reduce_scatter | solution.py:117
  114.5 31.6 %copy-start = (f32[128,1024]{1,0:T(8,128)S(1)}, f32[128,1024]{1,0:T(8,128)}, u32[]{:S(2)}) copy-start(f32[128,1024]{1,0:T(8,128)} %param.9) | copy-start | bytes 1572868
  116.3 32.2 %copy-start.3 = (f32[128,1024]{1,0:T(8,128)S(1)}, f32[128,1024]{1,0:T(8,128)}, u32[]{:S(2)}) copy-start(f32[128,1024]{1,0:T(8,128)} %param.17) | copy-start | bytes 1572868
  116.3 81.1 %all-gather.15.cloned.1.call-start = ((), (), s32[]{:S(2)}) async-start(), calls=%async_computation.14 | async-start | bytes 2359296 | tf_op jit(solution)/shard_map/all_gather | solution.py:122
  116.9 97.8 %all-gather.13.cloned.1.call-start = ((), (), s32[]{:S(2)}) async-start(), calls=%async_computation.13 | async-start | bytes 1310720 | tf_op jit(solution)/shard_map/all_gather | solution.py:120
  148.4 85.0 %all-gather.19.cloned.1.call-start = ((), (), s32[]{:S(2)}) async-start(), calls=%async_computation.17 | async-start | bytes 1310720 | tf_op jit(solution)/shard_map/all_gather | solution.py:134
  149.3 136.6 %all-gather.17.cloned.1.call-start = ((), (), s32[]{:S(2)}) async-start(), calls=%async_computation.15 | async-start | bytes 2359296 | tf_op jit(solution)/shard_map/all_gather | solution.py:124
  150.0 174.5 %reduce-scatter.20.cloned.1.call-start = ((), (), s32[]{:S(2)}) async-start(), calls=%async_computation.18 | async-start | bytes 2621440 | tf_op jit(solution)/shard_map/reduce_scatter | solution.py:143
  295.0 63.3 %reduce-scatter.18.cloned.1.call-start = ((), (), s32[]{:S(2)}) async-start(), calls=%async_computation.16 | async-start | bytes 2621440 | tf_op jit(solution)/shard_map/reduce_scatter | solution.py:131
  300.3 78.0 %all-gather.21.cloned.1.call-start = ((), (), s32[]{:S(2)}) async-start(), calls=%async_computation.19 | async-start | bytes 1310720 | tf_op jit(solution)/shard_map/all_gather | solution.py:148
  361.4 61.0 %reduce-scatter.22.cloned.1.call-start = ((), (), s32[]{:S(2)}) async-start(), calls=%async_computation.20 | async-start | bytes 2621440 | tf_op jit(solution)/shard_map/reduce_scatter | solution.py:161
  391.1 33.9 %copy-start.16 = (bf16[512,1024]{1,0:T(8,128)(2,1)S(1)}, bf16[512,1024]{1,0:T(8,128)(2,1)}, u32[]{:S(2)}) copy-start(bf16[512,1024]{1,0:T(8,128)(2,1)} %all-gather.9.cloned.1.call-done) | copy-start | bytes 3145732
  391.1 96.9 %reduce-scatter.32.cloned.1.call-start = ((), (), s32[]{:S(2)}) async-start(), calls=%async_computation.25 | async-start | bytes 147456
  392.0 233.2 %reduce-scatter.34.cloned.1.call-start = ((), (), s32[]{:S(2)}) async-start(), calls=%async_computation.26 | async-start | bytes 540672
  424.9 274.6 %reduce-scatter.24.cloned.1.call-start = ((), (), s32[]{:S(2)}) async-start(), calls=%async_computation.21 | async-start | bytes 3538944 | tf_op jit(solution)/shard_map/reduce_scatter | solution.py:177
  427.7 339.6 %reduce-scatter.26.cloned.1.call-start = ((), (), s32[]{:S(2)}) async-start(), calls=%async_computation.22 | async-start | bytes 1179648 | tf_op jit(solution)/shard_map/reduce_scatter | solution.py:179
  430.4 428.7 %reduce-scatter.30.cloned.1.call-start = ((), (), s32[]{:S(2)}) async-start(), calls=%async_computation.24 | async-start | bytes 4718592 | tf_op jit(solution)/shard_map/reduce_scatter | solution.py:182
  435.6 515.5 %reduce-scatter.28.cloned.1.call-start = ((), (), s32[]{:S(2)}) async-start(), calls=%async_computation.23 | async-start | bytes 4718592 | tf_op jit(solution)/shard_map/reduce_scatter | solution.py:180
  440.3 69.2 %copy-start.4 = (f32[128,1024]{1,0:T(8,128)S(1)}, f32[128,1024]{1,0:T(8,128)}, u32[]{:S(2)}) copy-start(f32[128,1024]{1,0:T(8,128)} %reduce-scatter.22.cloned.1.call-done) | copy-start | bytes 1572868
  (12 other events, 30.3 us)
Sparse Core Ops, SparseCore 0:
  39.9 15.9 all-gather.8
  58.5 48.7 all-gather.10
  116.4 29.6 reduce-scatter.15
  148.1 49.2 all-gather.14
  199.4 15.2 all-gather.12
  216.7 16.6 all-gather.18
  235.4 50.3 all-gather.16
  295.1 29.3 reduce-scatter.19
  327.1 31.1 reduce-scatter.17
  361.5 16.6 all-gather.20
  391.2 31.1 reduce-scatter.21
  426.1 61.8 reduce-scatter.31
  490.2 134.8 reduce-scatter.33
  628.6 70.7 reduce-scatter.23
  703.3 64.0 reduce-scatter.25
  771.4 87.6 reduce-scatter.29
  863.1 87.9 reduce-scatter.27
where the time goes:
time: 958 us
  waiting for transfers between devices  734 us (77%)
  blocking collectives  128 us (13%)
  matrix products  49.4 us (5%)
  other arithmetic  15.3 us (2%)
  between operations  14.9 us (2%)
  local copies, waits for them, and re-layouts  14.8 us (2%)
    unnamed x19, waiting for transfers between devices  162 us
    reduce_scatter x1, waiting for transfers between devices, body(): lax.psum_scatter(grad_up, 'dp', scatter_dimension=0, tiled=True)  92 us
    reduce_scatter x1, waiting for transfers between devices, body(): lax.psum_scatter(grad_down, 'dp', scatter_dimension=1, tiled=True)  91.7 us
    reduce_scatter x1, waiting for transfers between devices, body(): lax.psum_scatter(grad_in_w, 'dp', scatter_dimension=1, tiled=True)  72.9 us
    reduce_scatter x1, waiting for transfers between devices, body(): lax.psum_scatter(grad_proj_out, 'dp', scatter_dimension=1, tiled=True)  66 us
    all_gather x1, waiting for transfers between devices, body(): lax.all_gather(down_proj, 'dp', axis=1, tiled=True)  52.4 us
    reduce_scatter x1, waiting for transfers between devices, body(): lax.psum_scatter(feed_part, 'tensor', scatter_dimension=0, tiled=True)  32.4 us
    all_gather x1, blocking collectives, body(): lax.all_gather(in_bias, 'dp', axis=2, tiled=True)  30.7 us
  transfers between devices with their start and end apart: 17, of which 16 were waited for; matrix products, arithmetic and copies ran while one was open for 4% of the time, Pallas kernels for 0%

commit v1 on v0

--- a/solution.py
+++ b/solution.py
@@ -1,9 +1,171 @@
+import functools
 import math
 
 import jax
 import jax.numpy as jnp
 from jax import lax
+from jax.experimental import pallas as pl
+from jax.experimental.pallas import tpu as pltpu
 from jax.sharding import PartitionSpec as P
+
+MESH = pl.DeviceIdType.MESH
+
+
+def greet(axis, peers):
+    barrier = pltpu.get_barrier_semaphore()
+    for peer in peers:
+        pl.semaphore_signal(barrier, inc=1, device_id={axis: peer}, device_id_type=MESH)
+    pl.semaphore_wait(barrier, len(peers))
+
+
+def send(axis, src, dst, send_sem, recv_sem, peer):
+    return pltpu.make_async_remote_copy(
+        src_ref=src,
+        dst_ref=dst,
+        send_sem=send_sem,
+        recv_sem=recv_sem,
+        device_id={axis: peer},
+        device_id_type=MESH,
+    )
+
+
+def gather_kernel(axis, n, x_ref, out_ref, send_sem, recv_sem, own_sem):
+    me = lax.axis_index(axis)
+    groups = n // 2
+    side, group = lax.rem(me, 2), me // 2
+    mate = group * 2 + 1 - side
+    across = [lax.rem(group + k, groups) * 2 + side for k in range(1, groups)]
+    behind = [lax.rem(group + groups - k, groups) * 2 + side for k in range(1, groups)]
+    greet(axis, [mate] + across)
+    own = pltpu.make_async_copy(x_ref, out_ref.at[me], own_sem)
+    own.start()
+    far = []
+    for k, peer in enumerate(across):
+        far.append(send(axis, x_ref, out_ref.at[me], send_sem.at[k], recv_sem.at[k], peer))
+        far[-1].start()
+    near = [send(axis, x_ref, out_ref.at[me], send_sem.at[groups], recv_sem.at[groups], mate)]
+    near[0].start()
+    for k, copy in enumerate(far):
+        copy.wait_recv()
+        at = groups + 1 + k
+        block = out_ref.at[behind[k]]
+        near.append(send(axis, block, block, send_sem.at[at], recv_sem.at[at], mate))
+        near[-1].start()
+    for copy in far:
+        copy.wait_send()
+    for copy in near:
+        copy.wait()
+    own.wait()
+
+
+def gather_rows(x, axis, n, collective_id):
+    rows, columns = x.shape
+    out = pl.pallas_call(
+        functools.partial(gather_kernel, axis, n),
+        out_shape=jax.ShapeDtypeStruct((n, rows, columns), x.dtype),
+        in_specs=[pl.BlockSpec(memory_space=pltpu.VMEM)],
+        out_specs=pl.BlockSpec(memory_space=pltpu.VMEM),
+        scratch_shapes=[
+            pltpu.SemaphoreType.DMA((n,)),
+            pltpu.SemaphoreType.DMA((n,)),
+            pltpu.SemaphoreType.DMA,
+        ],
+        compiler_params=pltpu.CompilerParams(collective_id=collective_id, has_side_effects=True),
+    )(x)
+    return out.reshape(n * rows, columns)
+
+
+def scatter_kernel(axis, n, x_ref, out_ref, got, mine, far_got, send_sem, recv_sem):
+    me = lax.axis_index(axis)
+    groups = n // 2
+    side, group = lax.rem(me, 2), me // 2
+    mate = group * 2 + 1 - side
+    across = [lax.rem(group + k, groups) * 2 + side for k in range(1, groups)]
+    greet(axis, [mate] + across)
+    near = []
+    for k in range(1, groups + 1):
+        there = lax.rem(group + k, groups)
+        block = x_ref.at[there * 2 + 1 - side]
+        near.append(send(axis, block, got.at[k - 1], send_sem.at[k - 1], recv_sem.at[k - 1], mate))
+        near[-1].start()
+    far = []
+    for k in range(1, groups):
+        near[k - 1].wait_recv()
+        there = lax.rem(group + k, groups)
+        both = x_ref[there * 2 + side].astype(jnp.float32) + got[k - 1].astype(jnp.float32)
+        mine[k - 1] = both.astype(mine.dtype)
+        at = groups + k
+        far.append(
+            send(axis, mine.at[k - 1], far_got.at[k - 1], send_sem.at[at], recv_sem.at[at], across[k - 1])
+        )
+        far[-1].start()
+    near[groups - 1].wait_recv()
+    out_ref[...] = x_ref[me].astype(jnp.float32) + got[groups - 1].astype(jnp.float32)
+    for k, copy in enumerate(far):
+        copy.wait_recv()
+        out_ref[...] += far_got[k].astype(jnp.float32)
+    for copy in near + far:
+        copy.wait_send()
+
+
+def scatter_rows(x, axis, n, collective_id):
+    rows, columns = x.shape
+    rows = rows // n
+    groups = n // 2
+    return pl.pallas_call(
+        functools.partial(scatter_kernel, axis, n),
+        out_shape=jax.ShapeDtypeStruct((rows, columns), jnp.float32),
+        in_specs=[pl.BlockSpec(memory_space=pltpu.VMEM)],
+        out_specs=pl.BlockSpec(memory_space=pltpu.VMEM),
+        scratch_shapes=[
+            pltpu.VMEM((groups, rows, columns), jnp.bfloat16),
+            pltpu.VMEM((max(groups - 1, 1), rows, columns), jnp.bfloat16),
+            pltpu.VMEM((max(groups - 1, 1), rows, columns), jnp.bfloat16),
+            pltpu.SemaphoreType.DMA((n,)),
+            pltpu.SemaphoreType.DMA((n,)),
+        ],
+        compiler_params=pltpu.CompilerParams(collective_id=collective_id, has_side_effects=True),
+    )(x.astype(jnp.bfloat16).reshape(n, rows, columns))
+
+
+def exchange_kernel(axis, n, whole, x_ref, out_ref, send_sem, recv_sem, own_sem):
+    me = lax.axis_index(axis)
+    peers = [lax.rem(me + k, n) for k in range(1, n)]
+    greet(axis, peers)
+    own = pltpu.make_async_copy(x_ref if whole else x_ref.at[me], out_ref.at[me], own_sem)
+    own.start()
+    copies = []
+    for k, peer in enumerate(peers):
+        src = x_ref if whole else x_ref.at[peer]
+        copies.append(send(axis, src, out_ref.at[me], send_sem.at[k], recv_sem.at[k], peer))
+        copies[-1].start()
+    for copy in copies:
+        copy.wait()
+    own.wait()
+
+
+def exchange(x, axis, n, collective_id, whole):
+    block = x.shape if whole else x.shape[1:]
+    return pl.pallas_call(
+        functools.partial(exchange_kernel, axis, n, whole),
+        out_shape=jax.ShapeDtypeStruct((n,) + block, x.dtype),
+        in_specs=[pl.BlockSpec(memory_space=pltpu.VMEM)],
+        out_specs=pl.BlockSpec(memory_space=pltpu.VMEM),
+        scratch_shapes=[
+            pltpu.SemaphoreType.DMA((n,)),
+            pltpu.SemaphoreType.DMA((n,)),
+            pltpu.SemaphoreType.DMA,
+        ],
+        compiler_params=pltpu.CompilerParams(collective_id=collective_id, has_side_effects=True),
+    )(x)
+
+
+def packed(parts, lead):
+    flat = jnp.concatenate([p.reshape(lead + (-1,)) for p in parts], -1)
+    size = flat.shape[-1]
+    room = -(-size // 2048) * 2048
+    flat = jnp.pad(flat, [(0, 0)] * len(lead) + [(0, room - size)])
+    return flat.reshape(lead + (room // 128, 128))
 
 
 def layer_norm(rows, gain, shift):
@@ -87,20 +249,26 @@
     return (grad_qs.reshape(seq_len, heads, head_dim), grad_k, grad_v)
 
 
-def body(block_in, in_proj, in_bias, out_proj, up_proj, up_bias, down_proj, norm_params, grad_out):
-    proj_in, bias_in, proj_out, norms = (
-        lax.all_gather(in_proj, "dp", axis=1, tiled=True),
-        lax.all_gather(in_bias, "dp", axis=2, tiled=True),
-        lax.all_gather(out_proj, "dp", axis=1, tiled=True),
-        lax.all_gather(norm_params, "dp", axis=1, tiled=True),
-    )
+def body(dp, tensor, block_in, in_proj, in_bias, out_proj, up_proj, up_bias, down_proj, norm_params, grad_out):
+    proj_in = lax.all_gather(in_proj, "dp", axis=1, tiled=True)
+    proj_out = lax.all_gather(out_proj, "dp", axis=1, tiled=True)
+    small = exchange(packed([norm_params, in_bias, up_bias], ()), "dp", dp, 0, True)
+    small = small.reshape(dp, -1)
+    ends = [norm_params.size, norm_params.size + in_bias.size]
+    ends.append(ends[1] + up_bias.size)
+    norms = small[:, : ends[0]].reshape((dp,) + norm_params.shape)
+    norms = norms.transpose(1, 0, 2).reshape(6, -1)
+    bias_in = small[:, ends[0] : ends[1]].reshape((dp,) + in_bias.shape)
+    bias_in = bias_in.transpose(1, 2, 0, 3).reshape(2, in_bias.shape[1], -1)
+    bias_up = small[:, ends[1] : ends[2]].reshape((dp,) + up_bias.shape)
+    bias_up = bias_up.transpose(1, 0, 2).reshape(up_bias.shape[0], -1)
     norms = norms.astype(jnp.float32)
     gain_one, shift_one, bias_attn, gain_two, shift_two, bias_feed = [norms[i] for i in range(6)]
     heads_here = bias_in.shape[1]
     head_dim = bias_in.shape[2]
     columns = heads_here * head_dim
     normed_one = layer_norm(block_in, gain_one, shift_one).astype(jnp.bfloat16)
-    whole_one = lax.all_gather(normed_one, "tensor", axis=0, tiled=True)
+    whole_one = gather_rows(normed_one, "tensor", tensor, 1)
     seq_len = whole_one.shape[0]
     projected = jnp.einsum("ld,jdc->jlc", whole_one, proj_in, preferred_element_type=jnp.float32)
     bias_flat = bias_in.astype(jnp.float32).reshape(2, columns)
@@ -114,24 +282,21 @@
     mixed, log_total = attend(query, keys, values)
     mixed_flat = mixed.reshape(seq_len, columns)
     attn_part = jnp.dot(mixed_flat, proj_out, preferred_element_type=jnp.float32)
-    attn_sum = lax.psum_scatter(attn_part, "tensor", scatter_dimension=0, tiled=True)
+    attn_sum = scatter_rows(attn_part, "tensor", tensor, 5)
     middle = block_in + attn_sum + bias_attn
     normed_two = layer_norm(middle, gain_two, shift_two).astype(jnp.bfloat16)
-    whole_two = lax.all_gather(normed_two, "tensor", axis=0, tiled=True)
-    proj_up, bias_up, proj_down = (
-        lax.all_gather(up_proj, "dp", axis=0, tiled=True),
-        lax.all_gather(up_bias, "dp", axis=1, tiled=True),
-        lax.all_gather(down_proj, "dp", axis=1, tiled=True),
-    )
+    whole_two = gather_rows(normed_two, "tensor", tensor, 2)
+    proj_up = lax.all_gather(up_proj, "dp", axis=0, tiled=True)
+    proj_down = lax.all_gather(down_proj, "dp", axis=1, tiled=True)
     hidden_pre = jnp.dot(whole_two, proj_up, preferred_element_type=jnp.float32) + bias_up.astype(
         jnp.float32
     ).reshape(-1)
     hidden = gelu_curve(hidden_pre).astype(jnp.bfloat16)
     feed_part = jnp.dot(hidden, proj_down, preferred_element_type=jnp.float32)
-    feed_sum = lax.psum_scatter(feed_part, "tensor", scatter_dimension=0, tiled=True)
+    feed_sum = scatter_rows(feed_part, "tensor", tensor, 6)
     block_out = middle + feed_sum + bias_feed
     grad_low = grad_out.astype(jnp.bfloat16)
-    whole_grad = lax.all_gather(grad_low, "tensor", axis=0, tiled=True)
+    whole_grad = gather_rows(grad_low, "tensor", tensor, 3)
     grad_down = jnp.einsum("lf,ld->fd", hidden, whole_grad, preferred_element_type=jnp.float32)
     grad_hidden = jnp.einsum("ld,fd->lf", whole_grad, proj_down, preferred_element_type=jnp.float32)
     _, curve_back = jax.vjp(gelu_curve, hidden_pre)
@@ -140,12 +305,12 @@
     grad_pre_low = grad_pre.astype(jnp.bfloat16)
     grad_up = jnp.einsum("ld,lf->df", whole_two, grad_pre_low, preferred_element_type=jnp.float32)
     two_part = jnp.einsum("lf,df->ld", grad_pre_low, proj_up, preferred_element_type=jnp.float32)
-    normed_two_grad = lax.psum_scatter(two_part, "tensor", scatter_dimension=0, tiled=True)
+    normed_two_grad = scatter_rows(two_part, "tensor", tensor, 7)
     _, norm_back_two = jax.vjp(layer_norm, middle, gain_two, shift_two)
     grad_mid_norm, grad_gain_two, grad_shift_two = norm_back_two(normed_two_grad)
     grad_middle = grad_out + grad_mid_norm
     middle_low = grad_middle.astype(jnp.bfloat16)
-    whole_mid = lax.all_gather(middle_low, "tensor", axis=0, tiled=True)
+    whole_mid = gather_rows(middle_low, "tensor", tensor, 4)
     grad_proj_out = jnp.einsum(
         "lc,ld->cd", mixed_flat, whole_mid, preferred_element_type=jnp.float32
     )
@@ -158,7 +323,7 @@
     )
     grad_in_w = jnp.einsum("ld,jlc->jdc", whole_one, grad_proj, preferred_element_type=jnp.float32)
     one_part = jnp.einsum("jlc,jdc->ld", grad_proj, proj_in, preferred_element_type=jnp.float32)
-    normed_one_grad = lax.psum_scatter(one_part, "tensor", scatter_dimension=0, tiled=True)
+    normed_one_grad = scatter_rows(one_part, "tensor", tensor, 8)
     _, norm_back_one = jax.vjp(layer_norm, block_in, gain_one, shift_one)
     grad_in_norm, grad_gain_one, grad_shift_one = norm_back_one(normed_one_grad)
     grad_in = grad_middle + grad_in_norm
@@ -172,16 +337,29 @@
             jnp.sum(grad_out, 0),
         ]
     )
-    grad_norms = lax.psum_scatter(norm_terms, ("dp", "tensor"), scatter_dimension=1, tiled=True)
-    summed = (
-        lax.psum_scatter(grad_in_w, "dp", scatter_dimension=1, tiled=True),
-        lax.psum_scatter(grad_bias_in, "dp", scatter_dimension=2, tiled=True),
-        lax.psum_scatter(grad_proj_out, "dp", scatter_dimension=1, tiled=True),
-        lax.psum_scatter(grad_up, "dp", scatter_dimension=0, tiled=True),
-        lax.psum_scatter(grad_upb, "dp", scatter_dimension=1, tiled=True),
-        lax.psum_scatter(grad_down, "dp", scatter_dimension=1, tiled=True),
-    )
-    grad_in_proj, grad_in_bias, grad_out_proj, grad_up_proj, grad_up_bias, grad_down_proj = summed
+    pieces = [
+        norm_terms.reshape(6, dp, -1).transpose(1, 0, 2),
+        grad_bias_in.reshape(in_bias.shape[:2] + (dp, -1)).transpose(2, 0, 1, 3),
+        grad_upb.reshape(up_bias.shape[0], dp, -1).transpose(1, 0, 2),
+    ]
+    pieces = [p.reshape(dp, -1) for p in pieces]
+    tiny = jnp.sum(exchange(packed(pieces, (dp,)), "dp", dp, 9, False), 0).reshape(-1)
+    grad_in_bias = tiny[ends[0] : ends[1]].reshape(in_bias.shape)
+    grad_up_bias = tiny[ends[1] : ends[2]].reshape(up_bias.shape)
+    quarter = tiny[: ends[0]].reshape(6, tensor, -1).transpose(1, 0, 2).reshape(tensor, -1)
+    width = quarter.shape[1]
+    quarter = jnp.sum(exchange(packed([quarter], (tensor,)), "tensor", tensor, 10, False), 0)
+    grad_norms = quarter.reshape(-1)[:width].reshape(6, -1)
+
+    def summed(array, axis):
+        return lax.psum_scatter(
+            array.astype(jnp.bfloat16), "dp", scatter_dimension=axis, tiled=True
+        ).astype(jnp.float32)
+
+    grad_in_proj = summed(grad_in_w, 1)
+    grad_out_proj = summed(grad_proj_out, 1)
+    grad_up_proj = summed(grad_up, 0)
+    grad_down_proj = summed(grad_down, 1)
     return (
         block_out,
         grad_in,
@@ -197,7 +375,7 @@
 
 def solution(mesh):
     return jax.shard_map(
-        body,
+        functools.partial(body, mesh.shape["dp"], mesh.shape["tensor"]),
         mesh=mesh,
         in_specs=(
             P(("dp", "tensor"), None),

time: 958 us -> 502 us (0.52)
  waiting for transfers between devices: 734 us -> 242 us
  Pallas kernels: 0 us -> 118 us
  blocking collectives: 128 us -> 29.9 us
  local copies, waits for them, and re-layouts: 14.8 us -> 27.9 us
    reduce_scatter x8 -> x1, waiting for transfers between devices: 439 us -> 69 us  [summed(): lax.psum_scatter(array.astype(jnp.bfloat16), 'dp', scatter_dimension=axis...]
    pallas_call x0 -> x11, Pallas kernels: none -> 118 us  [the longest x4 48.8 us: scatter_rows(): pl.pallas_call(functools.partial(scatter_kernel, axis, n), out_shape=jax....]
    all_gather x7 -> x3, waiting for transfers between devices: 134 us -> 43.5 us  [the longest x1 43.4 us: body(): proj_down = lax.all_gather(down_proj, 'dp', axis=1, tiled=True)]
    all_gather x4 -> x1, blocking collectives: 109 us -> 29.9 us  [body(): proj_out = lax.all_gather(out_proj, 'dp', axis=1, tiled=True)]
    unnamed x19 -> x10, waiting for transfers between devices: 162 us -> 129 us
    unnamed x1 -> x0, blocking collectives: 19.5 us -> none
    unnamed x48 -> x59, local copies, waits for them, and re-layouts: 14 us -> 20.2 us
  transfers between devices with their start and end apart: 17 -> 7, of which waited for: 16 -> 4; matrix products, arithmetic and copies ran while one was open for 4% -> 14% of each run, Pallas kernels for 0% -> 16%
where the time goes in v1:
time: 502 us; the launch traced here: 501 us
  waiting for transfers between devices  242 us (48%)
  Pallas kernels  118 us (24%)
  matrix products  49.1 us (10%)
  blocking collectives  29.9 us (6%)
  local copies, waits for them, and re-layouts  27.9 us (6%)
  other arithmetic  18.4 us (4%)
  between operations  14.7 us (3%)
    unnamed x10, waiting for transfers between devices  129 us
    reduce_scatter x1, waiting for transfers between devices, summed(): lax.psum_scatter(array.astype(jnp.bfloat16), 'dp', scatter_dimension=axis...  69 us
    pallas_call x4, Pallas kernels, scatter_rows(): pl.pallas_call(functools.partial(scatter_kernel, axis, n), out_shape=jax....  48.8 us
    pallas_call x4, Pallas kernels, gather_rows(): pl.pallas_call(functools.partial(gather_kernel, axis, n), out_shape=jax.S...  46.5 us
    all_gather x1, waiting for transfers between devices, body(): proj_down = lax.all_gather(down_proj, 'dp', axis=1, tiled=True)  43.4 us
    all_gather x1, blocking collectives, body(): proj_out = lax.all_gather(out_proj, 'dp', axis=1, tiled=True)  29.9 us
    pallas_call x3, Pallas kernels, exchange(): pl.pallas_call(functools.partial(exchange_kernel, axis, n, whole), out_sh...  23 us
    unnamed x59, local copies, waits for them, and re-layouts  20.2 us
  transfers between devices with their start and end apart: 7, of which 4 were waited for; matrix products, arithmetic and copies ran while one was open for 14% of the time, Pallas kernels for 16%

profile of v1, /device:TPU:0, one launch (start us, length us, event | category | flops | bytes accessed | tf_op | source)
XLA Modules:
  0.0 500.5 jit_solution(2483006875176247809)
XLA Ops:
  13.5 9.8 %shard_map.160 = bf16[8,16,128]{2,1,0:T(8,128)(2,1)} custom-call(bf16[16,128]{1,0:T(8,128)(2,1)} %fusion.28.x_ref), custom_call_target="tpu_custom_call" | custom-call | tf_op jit(solution)/shard_map/pallas_call | solution.py:149
  26.8 29.9 %all_gather.13 = bf16[256,1024]{1,0:T(8,128)(2,1)S(1)} all-gather(bf16[256,128]{1,0:T(8,128)(2,1)S(1)} %copy-done.16), channel_id=1, replica_groups=mesh['dp'=8,'tensor'=4] {'dp'}, dimensions={1}, use_global_device_ids=true | all-gather | bytes 589824 | tf_op jit(solution)/shard_map/all_gather | solution.py:254
  57.6 11.6 %shard_map.161 = bf16[4,128,1024]{2,1,0:T(8,128)(2,1)} custom-call(bf16[128,1024]{1,0:T(8,128)(2,1)} %add_convert_fusion.3.x_ref), custom_call_target="tpu_custom_call" | custom-call | tf_op jit(solution)/shard_map/pallas_call | solution.py:63
  69.2 11.8 %shard_map.165 = bf16[4,128,1024]{2,1,0:T(8,128)(2,1)} custom-call(bf16[128,1024]{1,0:T(8,128)(2,1)} %get-tuple-element.121.x_ref), custom_call_target="tpu_custom_call" | custom-call | tf_op jit(solution)/shard_map/pallas_call | solution.py:63
  90.4 12.4 %shard_map.162 = f32[128,1024]{1,0:T(8,128)} custom-call(bf16[4,128,1024]{2,1,0:T(8,128)(2,1)} %bitcast.140), custom_call_target="tpu_custom_call" | custom-call | tf_op jit(solution)/shard_map/pallas_call | solution.py:115
  105.1 11.5 %shard_map.163 = bf16[4,128,1024]{2,1,0:T(8,128)(2,1)} custom-call(bf16[128,1024]{1,0:T(8,128)(2,1)} %add_convert_fusion.x_ref), custom_call_target="tpu_custom_call" | custom-call | tf_op jit(solution)/shard_map/pallas_call | solution.py:63
  116.7 4.5 fusion.49
  121.2 43.4 %all-gather.8.cloned.1.call-done = bf16[1024,1024]{1,0:T(8,128)(2,1)} async-done(((bf16[1024,128]{1,0:T(8,128)(2,1)}), bf16[1024,1024]{1,0:T(8,128)(2,1)}) %all-gather.8.cloned.1.call-update) | async-done | bytes 2097168 | tf_op jit(solution)/shard_map/all_gather | solution.py:290
  164.6 5.5 %fusion.39 = (f32[1024]{0:T(1024)S(1)}, bf16[512,1024]{1,0:T(8,128)(2,1)S(1)}) fusion(f32[512,1024]{1,0:T(8,128)} %fusion.49, f32[1024]{0:T(1024)S(1)} %reshape.301, bf16[512,1024]{1,0:T(8,128)(2,1)} %bitcast.146, bf16[1024,1024]{1,0:T(8,128)(2,1)} %all-gather.8.cloned.1.call-done), kind=kOutput, calls=%fused_computation.113 | convolution fusion | flops 1087372288 | bytes 6299648 | tf_op jit(solution)/shard_map/ld,fd->lf/dot_general | solution.py:301
  172.5 12.2 %shard_map.166 = f32[128,1024]{1,0:T(8,128)} custom-call(bf16[4,128,1024]{2,1,0:T(8,128)(2,1)} %bitcast.156), custom_call_target="tpu_custom_call" | custom-call | tf_op jit(solution)/shard_map/pallas_call | solution.py:115
  184.8 4.9 convolution_convert_fusion.4
  189.6 11.9 %shard_map.164 = f32[128,1024]{1,0:T(8,128)} custom-call(bf16[4,128,1024]{2,1,0:T(8,128)(2,1)} %bitcast.157), custom_call_target="tpu_custom_call" | custom-call | tf_op jit(solution)/shard_map/pallas_call | solution.py:115
  205.6 11.5 %shard_map.167 = bf16[4,128,1024]{2,1,0:T(8,128)(2,1)} custom-call(bf16[128,1024]{1,0:T(8,128)(2,1)} %convert_element_type.165.x_ref), custom_call_target="tpu_custom_call" | custom-call | tf_op jit(solution)/shard_map/pallas_call | solution.py:63
  221.5 4.2 multiply_convert_fusion
  231.2 3.8 fusion.47
  237.4 2.9 copy.104
  241.9 3.5 convolution_convert_fusion
  252.4 3.4 bitcast_convert_fusion
  255.7 12.2 %shard_map.168 = f32[128,1024]{1,0:T(8,128)} custom-call(bf16[4,128,1024]{2,1,0:T(8,128)(2,1)} %bitcast.155), custom_call_target="tpu_custom_call" | custom-call | tf_op jit(solution)/shard_map/pallas_call | solution.py:115
  270.4 8.1 %shard_map.169 = f32[8,16,128]{2,1,0:T(8,128)} custom-call(f32[8,16,128]{2,1,0:T(8,128)} %bitcast.162), custom_call_target="tpu_custom_call" | custom-call | tf_op jit(solution)/shard_map/pallas_call | solution.py:149
  280.4 5.1 %shard_map.170 = f32[4,16,128]{2,1,0:T(8,128)} custom-call(f32[4,16,128]{2,1,0:T(8,128)} %bitcast.165), custom_call_target="tpu_custom_call" | custom-call | tf_op jit(solution)/shard_map/pallas_call | solution.py:149
  291.0 58.9 %reduce-scatter.13.cloned.1.call-done = bf16[128,768]{1,0:T(8,128)(2,1)} async-done(((bf16[1024,768]{1,0:T(8,128)(2,1)}), bf16[128,768]{1,0:T(8,128)(2,1)}) %reduce-scatter.13.cloned.1.call-update) | async-done | bytes 196624
  352.0 68.9 %reduce-scatter.17.cloned.1.call-done = bf16[128,1024]{1,0:T(8,128)(2,1)} async-done(((bf16[1024,1024]{1,0:T(8,128)(2,1)}), bf16[128,1024]{1,0:T(8,128)(2,1)}) %reduce-scatter.17.cloned.1.call-update) | async-done | bytes 262160
  422.9 69.0 %reduce-scatter.11.cloned.1.call-done = bf16[128,1024]{1,0:T(8,128)(2,1)} async-done(((bf16[1024,1024]{1,0:T(8,128)(2,1)}), bf16[128,1024]{1,0:T(8,128)(2,1)}) %reduce-scatter.11.cloned.1.call-update) | async-done | bytes 262160 | tf_op jit(solution)/shard_map/reduce_scatter | solution.py:355
  (156 shorter events, 64.7 us)
Async XLA Ops:
  7.2 18.2 %copy-start = (f32[128,1024]{1,0:T(8,128)S(1)}, f32[128,1024]{1,0:T(8,128)}, u32[]{:S(2)}) copy-start(f32[128,1024]{1,0:T(8,128)} %param.9) | copy-start | bytes 1572868
  7.2 18.9 %copy-start.9 = (f32[128,1024]{1,0:T(8,128)S(1)}, f32[128,1024]{1,0:T(8,128)}, u32[]{:S(2)}) copy-start(f32[128,1024]{1,0:T(8,128)} %param.17) | copy-start | bytes 1572868
  7.2 19.6 %copy-start.16 = (bf16[256,128]{1,0:T(8,128)(2,1)S(1)}, bf16[256,128]{1,0:T(8,128)(2,1)}, u32[]{:S(2)}) copy-start(bf16[256,128]{1,0:T(8,128)(2,1)} %param.12) | copy-start | bytes 196612
  7.2 73.8 %all-gather.4.cloned.1.call-start = ((), (), s32[]{:S(2)}) async-start(), calls=%async_computation.4 | async-start | bytes 1769472 | tf_op jit(solution)/shard_map/all_gather | solution.py:253
  9.1 107.6 %all-gather.6.cloned.1.call-start = ((), (), s32[]{:S(2)}) async-start(), calls=%async_computation.5 | async-start | bytes 2359296 | tf_op jit(solution)/shard_map/all_gather | solution.py:289
  9.9 154.8 %all-gather.8.cloned.1.call-start = ((), (), s32[]{:S(2)}) async-start(), calls=%async_computation.6 | async-start | bytes 2359296 | tf_op jit(solution)/shard_map/all_gather | solution.py:290
  10.6 278.8 %reduce-scatter.15.cloned.1.call-start = ((), (), s32[]{:S(2)}) async-start(), calls=%async_computation.9 | async-start | bytes 589824
  84.0 1.9 copy-start.14
  84.9 1.9 copy-start.1
  164.6 5.6 %copy-start.17 = (bf16[1024,1024]{1,0:T(8,128)(2,1)S(1)}, bf16[1024,1024]{1,0:T(8,128)(2,1)}, u32[]{:S(2)}) copy-start(bf16[1024,1024]{1,0:T(8,128)(2,1)} %all-gather.6.cloned.1.call-done) | copy-start | bytes 6291460
  170.2 2.4 copy-start.18
  184.8 16.8 %copy-start.5 = (f32[128,1024]{1,0:T(8,128)S(1)}, f32[128,1024]{1,0:T(8,128)}, u32[]{:S(2)}) copy-start(f32[128,1024]{1,0:T(8,128)} %shard_map.166) | copy-start | bytes 1572868
  203.9 13.2 %copy-start.11 = (bf16[4,64,512]{2,1,0:T(8,128)(2,1)S(1)}, bf16[4,64,512]{2,1,0:T(8,128)(2,1)}, u32[]{:S(2)}) copy-start(bf16[4,64,512]{2,1,0:T(8,128)(2,1)} %copy-done.10) | copy-start | bytes 786436
  217.2 2.5 copy-start.6
  221.2 128.7 %reduce-scatter.13.cloned.1.call-start = ((), (), s32[]{:S(2)}) async-start(), calls=%async_computation.8 | async-start | bytes 1769472
  221.4 4.2 copy-start.8
  231.2 4.0 copy-start.12
  231.2 4.0 copy-start.15
  241.9 179.0 %reduce-scatter.17.cloned.1.call-start = ((), (), s32[]{:S(2)}) async-start(), calls=%async_computation.10 | async-start | bytes 2359296
  248.0 1.2 copy-start.13
  248.0 1.6 copy-start.19
  248.1 243.8 %reduce-scatter.11.cloned.1.call-start = ((), (), s32[]{:S(2)}) async-start(), calls=%async_computation.7 | async-start | bytes 2359296 | tf_op jit(solution)/shard_map/reduce_scatter | solution.py:355
  268.0 20.2 %copy-start.2 = (f32[128,1024]{1,0:T(8,128)S(1)}, f32[128,1024]{1,0:T(8,128)}, u32[]{:S(2)}) copy-start(f32[128,1024]{1,0:T(8,128)} %shard_map.168) | copy-start | bytes 1572868
  268.0 20.4 %copy-start.4 = (f32[128,1024]{1,0:T(8,128)S(1)}, f32[128,1024]{1,0:T(8,128)}, u32[]{:S(2)}) copy-start(f32[128,1024]{1,0:T(8,128)} %copy-done.3) | copy-start | bytes 1572868
  (3 other events, 2.6 us)
Sparse Core Ops, SparseCore 0:
  10.6 52.1 all-gather.3
  65.0 48.5 all-gather.5
  115.7 48.8 all-gather.7
  221.3 60.7 reduce-scatter.14
  285.3 64.5 reduce-scatter.12
  353.3 67.5 reduce-scatter.16
  424.4 67.4 reduce-scatter.10

commit v2 on v1

--- a/solution.py
+++ b/solution.py
@@ -251,7 +251,8 @@
 
 def body(dp, tensor, block_in, in_proj, in_bias, out_proj, up_proj, up_bias, down_proj, norm_params, grad_out):
     proj_in = lax.all_gather(in_proj, "dp", axis=1, tiled=True)
-    proj_out = lax.all_gather(out_proj, "dp", axis=1, tiled=True)
+    proj_out = gather_rows(out_proj, "dp", dp, 11).reshape((dp,) + out_proj.shape)
+    proj_out = proj_out.transpose(1, 0, 2).reshape(out_proj.shape[0], -1)
     small = exchange(packed([norm_params, in_bias, up_bias], ()), "dp", dp, 0, True)
     small = small.reshape(dp, -1)
     ends = [norm_params.size, norm_params.size + in_bias.size]
@@ -305,6 +306,9 @@
     grad_pre_low = grad_pre.astype(jnp.bfloat16)
     grad_up = jnp.einsum("ld,lf->df", whole_two, grad_pre_low, preferred_element_type=jnp.float32)
     two_part = jnp.einsum("lf,df->ld", grad_pre_low, proj_up, preferred_element_type=jnp.float32)
+    grad_down = grad_down.astype(jnp.bfloat16)
+    two_part, grad_down = lax.optimization_barrier((two_part.astype(jnp.bfloat16), grad_down))
+    down_sum = lax.psum_scatter(grad_down, "dp", scatter_dimension=1, tiled=True)
     normed_two_grad = scatter_rows(two_part, "tensor", tensor, 7)
     _, norm_back_two = jax.vjp(layer_norm, middle, gain_two, shift_two)
     grad_mid_norm, grad_gain_two, grad_shift_two = norm_back_two(normed_two_grad)
@@ -323,6 +327,7 @@
     )
     grad_in_w = jnp.einsum("ld,jlc->jdc", whole_one, grad_proj, preferred_element_type=jnp.float32)
     one_part = jnp.einsum("jlc,jdc->ld", grad_proj, proj_in, preferred_element_type=jnp.float32)
+    one_part, down_sum = lax.optimization_barrier((one_part.astype(jnp.bfloat16), down_sum))
     normed_one_grad = scatter_rows(one_part, "tensor", tensor, 8)
     _, norm_back_one = jax.vjp(layer_norm, block_in, gain_one, shift_one)
     grad_in_norm, grad_gain_one, grad_shift_one = norm_back_one(normed_one_grad)
@@ -351,15 +356,12 @@
     quarter = jnp.sum(exchange(packed([quarter], (tensor,)), "tensor", tensor, 10, False), 0)
     grad_norms = quarter.reshape(-1)[:width].reshape(6, -1)
 
-    def summed(array, axis):
-        return lax.psum_scatter(
-            array.astype(jnp.bfloat16), "dp", scatter_dimension=axis, tiled=True
-        ).astype(jnp.float32)
-
-    grad_in_proj = summed(grad_in_w, 1)
-    grad_out_proj = summed(grad_proj_out, 1)
-    grad_up_proj = summed(grad_up, 0)
-    grad_down_proj = summed(grad_down, 1)
+    blocks = grad_in_w.astype(jnp.bfloat16).reshape(3, dp, -1, columns).transpose(1, 0, 2, 3)
+    grad_in_proj = scatter_rows(blocks.reshape(-1, columns), "dp", dp, 12).reshape(in_proj.shape)
+    blocks = grad_proj_out.astype(jnp.bfloat16).reshape(columns, dp, -1).transpose(1, 0, 2)
+    grad_out_proj = scatter_rows(blocks.reshape(dp * columns, -1), "dp", dp, 13)
+    grad_up_proj = scatter_rows(grad_up, "dp", dp, 14)
+    grad_down_proj = down_sum.astype(jnp.float32)
     return (
         block_out,
         grad_in,

time: 502 us -> 373 us (0.74)
  waiting for transfers between devices: 242 us -> 52.1 us
  Pallas kernels: 118 us -> 212 us
  blocking collectives: 29.9 us -> 0 us
    unnamed x10 -> x5, waiting for transfers between devices: 129 us -> 1.41 us
    pallas_call x4 -> x7, Pallas kernels: 48.8 us -> 123 us  [scatter_rows(): pl.pallas_call(functools.partial(scatter_kernel, axis, n), out_shape=jax....]
    reduce_scatter x1 -> x0, waiting for transfers between devices: 69 us -> none  [summed(): lax.psum_scatter(array.astype(jnp.bfloat16), 'dp', scatter_dimension=axis...]
    all_gather x1 -> x0, blocking collectives: 29.9 us -> none  [body(): proj_out = lax.all_gather(out_proj, 'dp', axis=1, tiled=True)]
    pallas_call x4 -> x5, Pallas kernels: 46.5 us -> 63.5 us  [gather_rows(): pl.pallas_call(functools.partial(gather_kernel, axis, n), out_shape=jax.S...]
    all_gather x1, waiting for transfers between devices: 0.02 us -> 7.33 us  [body(): proj_up = lax.all_gather(up_proj, 'dp', axis=0, tiled=True)]
    unnamed x59 -> x71, local copies, waits for them, and re-layouts: 20.2 us -> 14.3 us
  transfers between devices with their start and end apart: 7 -> 4, of which waited for: 4 -> 2; matrix products, arithmetic and copies ran while one was open for 14% -> 17% of each run, Pallas kernels for 16% -> 46%
where the time goes in v2:
time: 373 us; the launch traced here: 371 us
  Pallas kernels  212 us (57%)
  waiting for transfers between devices  52.1 us (14%)
  matrix products  46 us (12%)
  local copies, waits for them, and re-layouts  30.4 us (8%)
  other arithmetic  16 us (4%)
  between operations  14.5 us (4%)
    pallas_call x7, Pallas kernels, scatter_rows(): pl.pallas_call(functools.partial(scatter_kernel, axis, n), out_shape=jax....  123 us
    pallas_call x5, Pallas kernels, gather_rows(): pl.pallas_call(functools.partial(gather_kernel, axis, n), out_shape=jax.S...  63.5 us
    all_gather x1, waiting for transfers between devices, body(): proj_down = lax.all_gather(down_proj, 'dp', axis=1, tiled=True)  43.4 us
    pallas_call x3, Pallas kernels, exchange(): pl.pallas_call(functools.partial(exchange_kernel, axis, n, whole), out_sh...  25.1 us
    unnamed x71, local copies, waits for them, and re-layouts  14.3 us
  transfers between devices with their start and end apart: 4, of which 2 were waited for; matrix products, arithmetic and copies ran while one was open for 17% of the time, Pallas kernels for 46%

profile of v2, /device:TPU:0, one launch (start us, length us, event | category | flops | bytes accessed | tf_op | source)
XLA Modules:
  0.0 371.0 jit_solution(7911257507460179935)
XLA Ops:
  13.5 9.8 %shard_map.160 = bf16[8,16,128]{2,1,0:T(8,128)(2,1)} custom-call(bf16[16,128]{1,0:T(8,128)(2,1)} %fusion.27.x_ref), custom_call_target="tpu_custom_call" | custom-call | tf_op jit(solution)/shard_map/pallas_call | solution.py:149
  26.8 16.6 %shard_map.162 = bf16[8,256,128]{2,1,0:T(8,128)(2,1)} custom-call(bf16[256,128]{1,0:T(8,128)(2,1)} %x_ref.1), custom_call_target="tpu_custom_call" | custom-call | tf_op jit(solution)/shard_map/pallas_call | solution.py:63
  45.5 11.7 %shard_map.161 = bf16[4,128,1024]{2,1,0:T(8,128)(2,1)} custom-call(bf16[128,1024]{1,0:T(8,128)(2,1)} %add_convert_fusion.3.x_ref), custom_call_target="tpu_custom_call" | custom-call | tf_op jit(solution)/shard_map/pallas_call | solution.py:63
  57.2 11.8 %shard_map.166 = bf16[4,128,1024]{2,1,0:T(8,128)(2,1)} custom-call(bf16[128,1024]{1,0:T(8,128)(2,1)} %get-tuple-element.84.x_ref), custom_call_target="tpu_custom_call" | custom-call | tf_op jit(solution)/shard_map/pallas_call | solution.py:63
  77.8 12.3 %shard_map.163 = f32[128,1024]{1,0:T(8,128)} custom-call(bf16[4,128,1024]{2,1,0:T(8,128)(2,1)} %bitcast.149), custom_call_target="tpu_custom_call" | custom-call | tf_op jit(solution)/shard_map/pallas_call | solution.py:115
  92.4 11.5 %shard_map.164 = bf16[4,128,1024]{2,1,0:T(8,128)(2,1)} custom-call(bf16[128,1024]{1,0:T(8,128)(2,1)} %add_convert_fusion.x_ref), custom_call_target="tpu_custom_call" | custom-call | tf_op jit(solution)/shard_map/pallas_call | solution.py:63
  103.8 7.3 %all-gather.6.cloned.1.call-done = bf16[1024,1024]{1,0:T(8,128)(2,1)} async-done(((bf16[128,1024]{1,0:T(8,128)(2,1)}), bf16[1024,1024]{1,0:T(8,128)(2,1)}) %all-gather.6.cloned.1.call-update) | async-done | bytes 2097168 | tf_op jit(solution)/shard_map/all_gather | solution.py:290
  111.2 3.2 fusion.48
  118.8 43.4 %all-gather.8.cloned.1.call-done = bf16[1024,1024]{1,0:T(8,128)(2,1)} async-done(((bf16[1024,128]{1,0:T(8,128)(2,1)}), bf16[1024,1024]{1,0:T(8,128)(2,1)}) %all-gather.8.cloned.1.call-update) | async-done | bytes 2097168 | tf_op jit(solution)/shard_map/all_gather | solution.py:291
  162.1 5.5 %fusion.38 = (f32[1024]{0:T(1024)S(1)}, bf16[512,1024]{1,0:T(8,128)(2,1)S(1)}) fusion(f32[512,1024]{1,0:T(8,128)} %copy-done.25, f32[1024]{0:T(1024)S(1)} %reshape.321, bf16[512,1024]{1,0:T(8,128)(2,1)} %bitcast.164, bf16[1024,1024]{1,0:T(8,128)(2,1)} %all-gather.8.cloned.1.call-done), kind=kOutput, calls=%fused_computation.112 | convolution fusion | flops 1087372288 | bytes 6299648 | tf_op jit(solution)/shard_map/ld,fd->lf/dot_general | solution.py:302
  170.0 12.2 %shard_map.167 = f32[128,1024]{1,0:T(8,128)} custom-call(bf16[4,128,1024]{2,1,0:T(8,128)(2,1)} %bitcast.170), custom_call_target="tpu_custom_call" | custom-call | tf_op jit(solution)/shard_map/pallas_call | solution.py:115
  182.2 4.0 %copy.116 = bf16[1024,1024]{0,1:T(8,128)(2,1)} copy(bf16[1024,1024]{1,0:T(8,128)(2,1)} %convolution_convert_fusion.1) | data formatting | bytes 4194304
  186.2 4.8 %convolution_convert_fusion.4 = bf16[512,1024]{1,0:T(8,128)(2,1)} fusion(bf16[1024,1024]{1,0:T(8,128)(2,1)} %all-gather.8.cloned.1.call-done, f32[512,1024]{1,0:T(8,128)} %copy-done.25, f32[1024]{0:T(1024)S(1)} %reshape.321), kind=kOutput, calls=%fused_computation.26 | convolution fusion | flops 1079508992 | bytes 5246976 | tf_op jit(solution)/shard_map/dot_general | solution.py:296
  191.2 12.1 %shard_map.165 = f32[128,1024]{1,0:T(8,128)} custom-call(bf16[4,128,1024]{2,1,0:T(8,128)(2,1)} %bitcast.169), custom_call_target="tpu_custom_call" | custom-call | tf_op jit(solution)/shard_map/pallas_call | solution.py:115
  207.3 12.0 %shard_map.168 = bf16[4,128,1024]{2,1,0:T(8,128)(2,1)} custom-call(bf16[128,1024]{1,0:T(8,128)(2,1)} %convert_element_type.157.x_ref), custom_call_target="tpu_custom_call" | custom-call | tf_op jit(solution)/shard_map/pallas_call | solution.py:63
  225.9 14.8 %shard_map.172 = f32[256,128]{1,0:T(8,128)} custom-call(bf16[8,256,128]{2,1,0:T(8,128)(2,1)} %bitcast.155), custom_call_target="tpu_custom_call" | custom-call | tf_op jit(solution)/shard_map/pallas_call | solution.py:115
  241.7 4.0 %multiply_convert_fusion = bf16[4,512,512]{1,2,0:T(8,128)(2,1)S(1)} fusion(f32[4,512,512]{1,2,0:T(8,128)} %copy-done.1, bf16[512,4,64]{0,2,1:T(8,128)(2,1)S(1)} %bitcast.176, f32[4,512]{1,0:T(4,128)S(1)} %bitcast.188, f32[4,512]{1,0:T(4,128)S(1)} %log_add_fusion, pred[512,512]{0,1:T(8,128)(4,1)S(1)} %iota_compare_fusion, f32[512,4,64]{0,2,1:T(8,128)S(1)} %bitcast.172, ...), kind=kOutput, calls=%fused_computation | convolution fusion | flops 141819904 | bytes 7357440 | tf_op jit(solution)/shard_map/while/body/eval_jaxpr/qhe,khe->hqk/dot_general | solution.py:229
  251.3 3.9 %fusion.46 = (f32[4,64]{1,0:T(4,128)S(1)}, bf16[512,4,64]{0,2,1:T(8,128)(2,1)S(1)}) fusion(bf16[512,4,64]{0,2,1:T(8,128)(2,1)} %bitcast.177, f32[4,512,512]{1,2,0:T(8,128)} %copy-done.1, f32[4,512]{1,0:T(4,128)S(1)} %log_add_fusion, pred[512,512]{0,1:T(8,128)(4,1)S(1)} %iota_compare_fusion), kind=kOutput, calls=%fused_computation.119 | convolution fusion | flops 139722496 | bytes 4989952 | tf_op jit(solution)/shard_map/while/body/eval_jaxpr/hqk,qhe->khe/dot_general | solution.py:226
  258.7 25.3 %shard_map.170 = f32[384,256]{1,0:T(8,128)} custom-call(bf16[8,384,256]{2,1,0:T(8,128)(2,1)} %bitcast.144), custom_call_target="tpu_custom_call" | custom-call | tf_op jit(solution)/shard_map/pallas_call | solution.py:115
  287.0 34.3 %shard_map.173 = f32[128,1024]{1,0:T(8,128)} custom-call(bf16[8,128,1024]{2,1,0:T(8,128)(2,1)} %bitcast.154), custom_call_target="tpu_custom_call" | custom-call | tf_op jit(solution)/shard_map/pallas_call | solution.py:115
  321.3 3.4 bitcast_convert_fusion
  325.8 12.3 %shard_map.169 = f32[128,1024]{1,0:T(8,128)} custom-call(bf16[4,128,1024]{2,1,0:T(8,128)(2,1)} %bitcast.168), custom_call_target="tpu_custom_call" | custom-call | tf_op jit(solution)/shard_map/pallas_call | solution.py:115
  340.3 10.3 %shard_map.171 = f32[8,16,128]{2,1,0:T(8,128)} custom-call(f32[8,16,128]{2,1,0:T(8,128)} %bitcast.175), custom_call_target="tpu_custom_call" | custom-call | tf_op jit(solution)/shard_map/pallas_call | solution.py:149
  352.8 5.1 %shard_map.174 = f32[4,16,128]{2,1,0:T(8,128)} custom-call(f32[4,16,128]{2,1,0:T(8,128)} %bitcast.180), custom_call_target="tpu_custom_call" | custom-call | tf_op jit(solution)/shard_map/pallas_call | solution.py:149
  (165 shorter events, 65.3 us)
Async XLA Ops:
  7.2 18.2 %copy-start = (f32[128,1024]{1,0:T(8,128)S(1)}, f32[128,1024]{1,0:T(8,128)}, u32[]{:S(2)}) copy-start(f32[128,1024]{1,0:T(8,128)} %param.9) | copy-start | bytes 1572868
  7.2 18.9 %copy-start.10 = (f32[128,1024]{1,0:T(8,128)S(1)}, f32[128,1024]{1,0:T(8,128)}, u32[]{:S(2)}) copy-start(f32[128,1024]{1,0:T(8,128)} %param.17) | copy-start | bytes 1572868
  7.2 61.8 %all-gather.4.cloned.1.call-start = ((), (), s32[]{:S(2)}) async-start(), calls=%async_computation.1 | async-start | bytes 1769472 | tf_op jit(solution)/shard_map/all_gather | solution.py:253
  9.1 102.1 %all-gather.6.cloned.1.call-start = ((), (), s32[]{:S(2)}) async-start(), calls=%async_computation.2 | async-start | bytes 2359296 | tf_op jit(solution)/shard_map/all_gather | solution.py:290
  9.8 152.3 %all-gather.8.cloned.1.call-start = ((), (), s32[]{:S(2)}) async-start(), calls=%async_computation.3 | async-start | bytes 2359296 | tf_op jit(solution)/shard_map/all_gather | solution.py:291
  10.6 314.1 %reduce-scatter.4.cloned.1.call-start = ((), (), s32[]{:S(2)}) async-start(), calls=%async_computation.4 | async-start | bytes 2359296
  111.2 4.6 %copy-start.15 = (bf16[4,128,1024]{2,1,0:T(8,128)(2,1)S(1)}, bf16[4,128,1024]{2,1,0:T(8,128)(2,1)}, u32[]{:S(2)}) copy-start(bf16[4,128,1024]{2,1,0:T(8,128)(2,1)} %shard_map.166) | copy-start | bytes 3145732
  162.1 5.6 %copy-start.24 = (bf16[1024,1024]{1,0:T(8,128)(2,1)S(1)}, bf16[1024,1024]{1,0:T(8,128)(2,1)}, u32[]{:S(2)}) copy-start(bf16[1024,1024]{1,0:T(8,128)(2,1)} %all-gather.6.cloned.1.call-done) | copy-start | bytes 6291460
  186.2 4.8 %copy-start.6 = (f32[128,1024]{1,0:T(8,128)S(1)}, f32[128,1024]{1,0:T(8,128)}, u32[]{:S(2)}) copy-start(f32[128,1024]{1,0:T(8,128)} %shard_map.167) | copy-start | bytes 1572868
  219.3 21.4 %copy-start.2 = (bf16[4,128,1024]{2,1,0:T(8,128)(2,1)S(1)}, bf16[4,128,1024]{2,1,0:T(8,128)(2,1)}, u32[]{:S(2)}) copy-start(bf16[4,128,1024]{2,1,0:T(8,128)(2,1)} %shard_map.168) | copy-start | bytes 3145732
  241.2 4.5 %copy-start.23 = (bf16[512,256]{0,1:T(8,128)(2,1)}, bf16[512,256]{0,1:T(8,128)(2,1)S(1)}, u32[]{:S(2)}) copy-start(bf16[512,256]{0,1:T(8,128)(2,1)S(1)} %get-tuple-element.102) | copy-start | bytes 786436
  241.7 4.0 %copy-start.8 = (bf16[1,512,256]{1,2,0:T(8,128)(2,1)S(1)}, bf16[1,512,256]{1,2,0:T(8,128)(2,1)}, u32[]{:S(2)}) copy-start(bf16[1,512,256]{1,2,0:T(8,128)(2,1)} %copy-done.7) | copy-start | bytes 786436
  251.3 4.0 %copy-start.21 = (bf16[1,512,256]{2,1,0:T(8,128)(2,1)}, bf16[1,512,256]{2,1,0:T(8,128)(2,1)S(1)}, u32[]{:S(2)}) copy-start(bf16[1,512,256]{2,1,0:T(8,128)(2,1)S(1)} %copy.99) | copy-start | bytes 786436
  251.3 4.0 %copy-start.13 = (bf16[4,128,1024]{2,1,0:T(8,128)(2,1)S(1)}, bf16[4,128,1024]{2,1,0:T(8,128)(2,1)}, u32[]{:S(2)}) copy-start(bf16[4,128,1024]{2,1,0:T(8,128)(2,1)} %shard_map.161) | copy-start | bytes 3145732
  251.3 4.0 %copy-start.19 = (bf16[1,512,256]{2,1,0:T(8,128)(2,1)S(1)}, bf16[1,512,256]{2,1,0:T(8,128)(2,1)}, u32[]{:S(2)}) copy-start(bf16[1,512,256]{2,1,0:T(8,128)(2,1)} %copy.98) | copy-start | bytes 786436
  256.8 27.5 %copy-start.14 = (bf16[4,128,1024]{2,1,0:T(8,128)(2,1)S(1)}, bf16[4,128,1024]{2,1,0:T(8,128)(2,1)}, u32[]{:S(2)}) copy-start(bf16[4,128,1024]{2,1,0:T(8,128)(2,1)} %shard_map.164) | copy-start | bytes 3145732
  258.7 25.6 %copy-start.27 = (bf16[512,1024]{1,0:T(8,128)(2,1)S(1)}, bf16[512,1024]{1,0:T(8,128)(2,1)}, u32[]{:S(2)}) copy-start(bf16[512,1024]{1,0:T(8,128)(2,1)} %copy-done.26) | copy-start | bytes 3145732
  287.0 34.3 %copy-start.20 = (bf16[1,512,256]{2,1,0:T(8,128)(2,1)S(1)}, bf16[1,512,256]{2,1,0:T(8,128)(2,1)}, u32[]{:S(2)}) copy-start(bf16[1,512,256]{2,1,0:T(8,128)(2,1)} %copy.98) | copy-start | bytes 786436
  287.0 34.3 %copy-start.22 = (bf16[1,512,256]{2,1,0:T(8,128)(2,1)S(1)}, bf16[1,512,256]{2,1,0:T(8,128)(2,1)}, u32[]{:S(2)}) copy-start(bf16[1,512,256]{2,1,0:T(8,128)(2,1)} %copy-done.21) | copy-start | bytes 786436
  338.1 13.6 %copy-start.3 = (f32[128,1024]{1,0:T(8,128)S(1)}, f32[128,1024]{1,0:T(8,128)}, u32[]{:S(2)}) copy-start(f32[128,1024]{1,0:T(8,128)} %shard_map.169) | copy-start | bytes 1572868
  338.1 23.3 %copy-start.5 = (f32[128,1024]{1,0:T(8,128)S(1)}, f32[128,1024]{1,0:T(8,128)}, u32[]{:S(2)}) copy-start(f32[128,1024]{1,0:T(8,128)} %copy-done.4) | copy-start | bytes 1572868
  351.7 10.6 %copy-start.12 = (f32[384,256]{1,0:T(8,128)S(1)}, f32[384,256]{1,0:T(8,128)}, u32[]{:S(2)}) copy-start(f32[384,256]{1,0:T(8,128)} %shard_map.170) | copy-start | bytes 1179652
  352.0 11.0 %copy-start.16 = (f32[256,128]{1,0:T(8,128)S(1)}, f32[256,128]{1,0:T(8,128)}, u32[]{:S(2)}) copy-start(f32[256,128]{1,0:T(8,128)} %shard_map.172) | copy-start | bytes 393220
  352.0 11.7 %copy-start.9 = (f32[128,1024]{1,0:T(8,128)S(1)}, f32[128,1024]{1,0:T(8,128)}, u32[]{:S(2)}) copy-start(f32[128,1024]{1,0:T(8,128)} %shard_map.173) | copy-start | bytes 1572868
  (8 other events, 12.5 us)
Sparse Core Ops, SparseCore 0:
  10.6 51.0 all-gather.3
  63.9 47.2 all-gather.5
  113.2 48.8 all-gather.7
  186.3 65.8 reduce-scatter.3
